TPU v7x, 512 devices: a whole 4x8x8 slice. The times are simulated.
512 devices in a mesh: seq: 128 (over z, y, core), head: 4 (over x).
Axes of the slice: x: 4, y: 8, z: 8, core: 2. Of those that a mesh axis runs over, the one named last changes fastest.
Arguments:
- features: bfloat16 [16384, 1024], P('seq'), may hold values from -6 to 6
- w_in: bfloat16 [1024, 1024], P(None, 'head'), may hold values from -0.1875 to 0.1875
- b_ahead: bfloat16 [16384, 128], P('seq'), may hold values from -6 to 6
- c_ahead: bfloat16 [16384, 128], P('seq'), may hold values from -0.015625 to 0.015625
- b_behind: bfloat16 [16384, 128], P('seq'), may hold values from -6 to 6
- c_behind: bfloat16 [16384, 128], P('seq'), may hold values from -0.015625 to 0.015625
- decay_ahead: float32 [16, 16384], P('head', 'seq'), may hold values from -2 to 0, as said below
- decay_behind: float32 [16, 16384], P('head', 'seq'), may hold values from -2 to 0, as said below
- skip_gain: float32 [16], P('head'), may hold values from 0.5 to 1.5
- grad_y: bfloat16 [16384, 1024], P('seq', 'head'), may hold values from -6 to 6
Outputs:
- grad_features: bfloat16 [16384, 1024], P('seq', 'head')
- grad_w_in: float32 [1024, 1024], P('seq', 'head')
- grad_b_ahead: float32 [16384, 128], P('seq')
- grad_c_ahead: float32 [16384, 128], P('seq')
- grad_b_behind: float32 [16384, 128], P('seq')
- grad_c_behind: float32 [16384, 128], P('seq')
- grad_decay_ahead: float32 [16, 16384], P('head', 'seq')
- grad_decay_behind: float32 [16, 16384], P('head', 'seq')
Inputs may be any that keep to these rules, and one draw needn't show every extreme that they name: `decay_ahead`: every log-decay is negative. `decay_behind`: every log-decay is negative.
All inputs are finite; a program needn't handle non-finite values.
Results may differ from a plain program's by a relative error of at most 0.039.
Values may be sent and summed in bfloat16 or wider, within the bound.
A program may use at most 128 MiB of HBM per device.

v0:
```python
import math

import jax
import jax.numpy as jnp
from jax import lax
from jax.sharding import PartitionSpec as P

HIGH = lax.Precision.HIGHEST
BF = jnp.bfloat16
F32 = jnp.float32


def dot(a, b, dims, precision=None):
    return lax.dot_general(a, b, dims, precision=precision, preferred_element_type=F32)


def triangle(n, lower):
    row = lax.broadcasted_iota(jnp.int32, (n, n), 0)
    col = lax.broadcasted_iota(jnp.int32, (n, n), 1)
    return (col <= row) if lower else (col >= row)


def running(d, lower):
    mask = triangle(d.shape[1], lower).astype(F32)
    return dot(d, mask, (((1,), (1,)), ((), ())), HIGH)


def three(v):
    high = v.astype(BF)
    rest = v - high.astype(F32)
    mid = rest.astype(BF)
    low = (rest - mid.astype(F32)).astype(BF)
    return [high, mid, low]


def chain(gain, lower):
    n = gain.shape[0]
    row = lax.broadcasted_iota(jnp.int32, (n, n), 0)
    col = lax.broadcasted_iota(jnp.int32, (n, n), 1)
    before = (col < row) if lower else (col > row)
    terms = jnp.where(before, gain[:, None], 0.0)
    strict = before.astype(F32)
    total = dot(strict, terms, (((1,), (0,)), ((), ())), HIGH)
    return jnp.where(before, jnp.exp(total), 0.0)


def edge(k, lower):
    return k[:, -1:] if lower else k[:, :1]


def summaries(x, g, b, c, k, lower):
    final = edge(k, lower)
    weight = jnp.exp(final - k)
    weighted = (x.astype(F32) * weight[:, :, None]).astype(BF)
    fresh = jnp.einsum("hsp,sn->hpn", weighted, b, preferred_element_type=F32)
    grown = (g.astype(F32) * jnp.exp(k)[:, :, None]).astype(BF)
    back = jnp.einsum("htp,tn->hpn", grown, c, preferred_element_type=F32)
    return weighted, weight, grown, fresh, back


def gradients(x, g, b, c, k, weighted, weight, grown, dscores, s_in, g_out, lower):
    n = k.shape[1]
    mask = triangle(n, lower)[None]
    spread = k[:, :, None] - k[:, None, :]
    decays = jnp.where(mask, jnp.exp(jnp.where(mask, spread, 0.0)), 0.0)
    aff = dot(c, b, (((1,), (1,)), ((), ())))
    scores32 = decays * aff[None]
    scores = scores32.astype(BF)
    grad_x = jnp.einsum("hts,htp->hsp", scores, g, preferred_element_type=F32)
    e = dscores * scores32
    daff = jnp.sum(dscores * decays, axis=0).astype(BF)
    grad_c = dot(daff, b, (((1,), (0,)), ((), ())))
    grad_b = dot(daff, c, (((0,), (0,)), ((), ())))
    dk = jnp.sum(e, axis=2) - jnp.sum(e, axis=1)
    dweighted = jnp.einsum("sn,hpn->hsp", b, g_out, preferred_element_type=F32)
    scaled = dweighted * weight[:, :, None]
    grad_x = grad_x + scaled
    u = jnp.sum(scaled * x.astype(F32), axis=2)
    grad_b = grad_b + jnp.einsum("hsp,hpn->sn", weighted, g_out, preferred_element_type=F32)
    grad_c = grad_c + jnp.einsum("htp,hpn->tn", grown, s_in, preferred_element_type=F32)
    carried = jnp.einsum("tn,hpn->htp", c, s_in, preferred_element_type=F32)
    dk = dk - u + jnp.exp(k) * jnp.sum(carried * g.astype(F32), axis=2)
    final = edge(k, lower)
    both = jnp.sum(g_out.astype(F32) * s_in.astype(F32), axis=(1, 2))[:, None]
    last = jnp.sum(u, axis=1, keepdims=True) + jnp.exp(final) * both
    grad_d = dot(dk, triangle(n, lower).astype(F32), (((1,), (0,)), ((), ())), HIGH) + last
    return grad_x, grad_b, grad_c, grad_d


def local(features, w_in, b_a, c_a, b_z, c_z, decay_a, decay_z, skip_gain, grad_y):
    frames = features.shape[0]
    heads = decay_a.shape[0]
    size = w_in.shape[1] // heads
    peers = lax.axis_size("seq")
    n = b_a.shape[1]
    x2 = jnp.dot(features, w_in, preferred_element_type=F32).astype(BF)
    x = x2.reshape(frames, heads, size).transpose(1, 0, 2)
    g = grad_y.reshape(frames, heads, size).transpose(1, 0, 2)
    k_a = running(decay_a, True)
    k_z = running(decay_z, False)
    wt_a, w_a, gr_a, f_a, q_a = summaries(x, g, b_a, c_a, k_a, True)
    wt_z, w_z, gr_z, f_z, q_z = summaries(x, g, b_z, c_z, k_z, False)
    per = heads * size // peers
    parts = [v.astype(BF).reshape(peers, per * n) for v in (f_a, q_a, f_z, q_z)]
    gains = three(jnp.sum(decay_a, axis=1)) + three(jnp.sum(decay_z, axis=1))
    gains = jnp.repeat(jnp.stack(gains, 1), peers // heads, axis=0)
    gains = jnp.pad(gains, ((0, 0), (0, n - gains.shape[1])))
    sent = jnp.concatenate(parts + [gains], axis=1)
    got = lax.all_to_all(sent, "seq", 0, 0, tiled=True)
    wide = per * n
    gain = got[:, 4 * wide :].astype(F32)
    t_a = chain(gain[:, 0] + gain[:, 1] + gain[:, 2], True)
    t_z = chain(gain[:, 3] + gain[:, 4] + gain[:, 5], False)
    got = got[:, : 4 * wide].astype(F32)
    plain = (((1,), (0,)), ((), ()))
    flip = (((0,), (0,)), ((), ()))
    back = [
        dot(t_a, got[:, :wide], plain, HIGH),
        dot(t_a, got[:, wide : 2 * wide], flip, HIGH),
        dot(t_z, got[:, 2 * wide : 3 * wide], plain, HIGH),
        dot(t_z, got[:, 3 * wide :], flip, HIGH),
    ]
    back = jnp.concatenate(back, axis=1).astype(BF)
    back = lax.all_to_all(back, "seq", 0, 0, tiled=True)
    s_a, o_a, s_z, o_z = [
        back[:, i * wide : (i + 1) * wide].reshape(heads, size, n) for i in range(4)
    ]
    dscores = jnp.einsum("htp,hsp->hts", g, x, preferred_element_type=F32).astype(BF).astype(F32)
    gx_a, gb_a, gc_a, gd_a = gradients(x, g, b_a, c_a, k_a, wt_a, w_a, gr_a, dscores, s_a, o_a, True)
    gx_z, gb_z, gc_z, gd_z = gradients(x, g, b_z, c_z, k_z, wt_z, w_z, gr_z, dscores, s_z, o_z, False)
    grad_x = gx_a + gx_z + skip_gain[:, None, None] * g.astype(F32)
    grad_x = grad_x.astype(BF).transpose(1, 0, 2).reshape(frames, heads * size)
    maps = jnp.concatenate([gb_a, gc_a, gb_z, gc_z], axis=1).astype(BF)
    maps = lax.psum(maps, "head").astype(F32)
    terms = dot(grad_x, w_in, (((1,), (1,)), ((), ()))).astype(BF)
    grad_features = lax.psum_scatter(terms, "head", scatter_dimension=1, tiled=True)
    weight_sum = lax.psum_scatter(
        dot(features, grad_x, flip), "seq", scatter_dimension=0, tiled=True
    )
    grad_w_in = weight_sum * (1.0 / math.sqrt(frames * peers))
    return (
        grad_features,
        grad_w_in,
        maps[:, :n],
        maps[:, n : 2 * n],
        maps[:, 2 * n : 3 * n],
        maps[:, 3 * n :],
        gd_a,
        gd_z,
    )


def solution(mesh):
    in_specs = (
        P("seq", None),
        P(None, "head"),
        P("seq", None),
        P("seq", None),
        P("seq", None),
        P("seq", None),
        P("head", "seq"),
        P("head", "seq"),
        P("head"),
        P("seq", "head"),
    )
    out_specs = (
        P("seq", "head"),
        P("seq", "head"),
        P("seq", None),
        P("seq", None),
        P("seq", None),
        P("seq", None),
        P("head", "seq"),
        P("head", "seq"),
    )
    return jax.shard_map(local, mesh=mesh, in_specs=in_specs, out_specs=out_specs, check_vma=False)
```

profile of v0, /device:TPU:1, one launch (start us, length us, event | category | flops | bytes accessed | tf_op | source)
XLA Modules:
  0.0 307.0 jit_solution(12466396961534745870)
XLA Ops:
  8.0 0.9 reduce_sum.148
  9.0 0.8 fusion.71
  10.7 0.6 copy-done.4
  11.4 0.7 copy-done.3
  12.7 0.6 copy-done.2
  13.6 0.7 copy-done.5
  14.6 0.5 broadcast.26
  15.1 0.8 reduce.14
  15.9 1.0 reshape.234
  16.9 18.4 %all-to-all-start = ((bf16[128,2,576]{2,1,0:T(2,128)(2,1)}), bf16[128,2,576]{2,1,0:T(2,128)(2,1)S(1)}, u32[]{:S(2)}, u32[]{:S(2)}) async-start(bf16[128,2,576]{2,1,0:T(2,128)(2,1)} %reshape.234), calls=%async_computation | async-start | bytes 655360 | tf_op jit(solution)/shard_map/all_to_all | solution.py:109
  35.7 0.5 fusion.33
  36.6 15.2 %all-to-all-done = bf16[128,2,576]{2,1,0:T(2,128)(2,1)S(1)} async-done(((bf16[128,2,576]{2,1,0:T(2,128)(2,1)}), bf16[128,2,576]{2,1,0:T(2,128)(2,1)S(1)}, u32[]{:S(2)}, u32[]{:S(2)}) %all-to-all-start) | async-done | bytes 294944 | tf_op jit(solution)/shard_map/all_to_all | solution.py:109
  54.2 0.8 reduce.15
  55.0 0.9 reshape.236
  55.9 5.5 %all-to-all-start.1 = ((bf16[128,2,512]{2,1,0:T(2,128)(2,1)}), bf16[128,2,512]{2,1,0:T(2,128)(2,1)S(1)}, u32[]{:S(2)}, u32[]{:S(2)}) async-start(bf16[128,2,512]{2,1,0:T(2,128)(2,1)} %reshape.236), calls=%async_computation.1 | async-start | bytes 524288 | tf_op jit(solution)/shard_map/all_to_all | solution.py:124
  61.9 14.8 %all-to-all-done.1 = bf16[128,2,512]{2,1,0:T(2,128)(2,1)S(1)} async-done(((bf16[128,2,512]{2,1,0:T(2,128)(2,1)}), bf16[128,2,512]{2,1,0:T(2,128)(2,1)S(1)}, u32[]{:S(2)}, u32[]{:S(2)}) %all-to-all-start.1) | async-done | bytes 262176 | tf_op jit(solution)/shard_map/all_to_all | solution.py:124
  78.3 0.7 pad_maximum_fusion.1
  79.6 0.7 copy-done.8
  80.8 1.3 copy.95
  83.6 1.0 convolution_convert_fusion
  84.6 0.8 convolution_add_fusion.1
  85.4 0.8 convolution_add_fusion
  86.2 35.3 %all-reduce.3.cloned.1.call-done = bf16[128,512]{0,1:T(8,128)(2,1)} async-done(((bf16[128,512]{0,1:T(8,128)(2,1)}), bf16[128,512]{0,1:T(8,128)(2,1)}) %all-reduce.3.cloned.1.call-update) | async-done | bytes 131088 | tf_op jit(solution)/shard_map/psum | solution.py:134
  121.4 0.8 fusion.110
  122.2 0.7 copy.90
  123.0 0.7 copy.89
  123.7 0.7 copy.88
  124.4 0.7 copy.87
  125.2 145.4 %reduce-scatter.7.cloned.1.call-done = f32[8,256]{1,0:T(8,128)} async-done(((f32[1024,256]{1,0:T(8,128)}), f32[8,256]{1,0:T(8,128)}) %reduce-scatter.7.cloned.1.call-update) | async-done | bytes 8208
  270.6 0.8 copy.96
  271.5 0.7 copy.86
  272.1 27.5 %reduce-scatter.5.cloned.1.call-done = bf16[128,256]{1,0:T(8,128)(2,1)} async-done(((bf16[128,1024]{1,0:T(8,128)(2,1)}), bf16[128,256]{1,0:T(8,128)(2,1)}) %reduce-scatter.5.cloned.1.call-update) | async-done | bytes 65552 | tf_op jit(solution)/shard_map/reduce_scatter | solution.py:136
  (92 shorter events, 9.7 us)
Async XLA Ops:
  8.0 4.3 %copy-start = (bf16[1024,256]{1,0:T(8,128)(2,1)S(1)}, bf16[1024,256]{1,0:T(8,128)(2,1)}, u32[]{:S(2)}) copy-start(bf16[1024,256]{1,0:T(8,128)(2,1)} %param.11) | copy-start | bytes 1572868
  8.0 0.9 copy-start.7
  8.0 2.4 copy-start.6
  10.5 0.8 copy-start.4
  11.2 1.1 copy-start.1
  11.4 0.8 copy-start.3
  12.6 0.8 copy-start.2
  13.5 0.8 copy-start.5
  16.9 35.0 %all-to-all-start = ((bf16[128,2,576]{2,1,0:T(2,128)(2,1)}), bf16[128,2,576]{2,1,0:T(2,128)(2,1)S(1)}, u32[]{:S(2)}, u32[]{:S(2)}) async-start(bf16[128,2,576]{2,1,0:T(2,128)(2,1)} %reshape.234), calls=%async_computation | async-start | bytes 655360 | tf_op jit(solution)/shard_map/all_to_all | solution.py:109
  55.9 20.9 %all-to-all-start.1 = ((bf16[128,2,512]{2,1,0:T(2,128)(2,1)}), bf16[128,2,512]{2,1,0:T(2,128)(2,1)S(1)}, u32[]{:S(2)}, u32[]{:S(2)}) async-start(bf16[128,2,512]{2,1,0:T(2,128)(2,1)} %reshape.236), calls=%async_computation.1 | async-start | bytes 524288 | tf_op jit(solution)/shard_map/all_to_all | solution.py:124
  61.4 60.0 %all-reduce.3.cloned.1.call-start = ((), (), s32[]{:S(2)}) async-start(), calls=%async_computation.5 | async-start | bytes 262144 | tf_op jit(solution)/shard_map/psum | solution.py:134
  79.0 191.6 %reduce-scatter.7.cloned.1.call-start = ((), (), s32[]{:S(2)}) async-start(), calls=%async_computation.6 | async-start | bytes 1056768
  79.6 0.7 copy-start.8
  82.2 217.4 %reduce-scatter.5.cloned.1.call-start = ((), (), s32[]{:S(2)}) async-start(), calls=%async_computation.4 | async-start | bytes 327680 | tf_op jit(solution)/shard_map/reduce_scatter | solution.py:136
Sparse Core Ops, SparseCore 0:
  79.1 42.2 all-reduce.2
Sparse Core Ops, SparseCore 1:
  83.8 186.8 reduce-scatter.6
  273.9 25.7 reduce-scatter.4
where the time goes:
time: 309 us; the launch traced here: 307 us
  waiting for transfers between devices  238 us (77%)
  starting transfers between devices  24.1 us (8%)
  between operations  15.9 us (5%)
  local copies, waits for them, and re-layouts  14.5 us (5%)
  matrix products  9.98 us (3%)
  other arithmetic  4.28 us (1%)
    unnamed x4, waiting for transfers between devices  145 us
    psum x1, waiting for transfers between devices, local(): maps = lax.psum(maps, 'head').astype(F32)  35.3 us
    reduce_scatter x1, waiting for transfers between devices, local(): lax.psum_scatter(terms, 'head', scatter_dimension=1, tiled=True)  27.5 us
    all_to_all x1, starting transfers between devices, local(): got = lax.all_to_all(sent, 'seq', 0, 0, tiled=True)  18.4 us
    all_to_all x1, waiting for transfers between devices, local(): got = lax.all_to_all(sent, 'seq', 0, 0, tiled=True)  15.2 us
    all_to_all x1, waiting for transfers between devices, local(): back = lax.all_to_all(back, 'seq', 0, 0, tiled=True)  14.8 us
    unnamed x36, local copies, waits for them, and re-layouts  11.9 us
    dot_general x18, matrix products, dot(): lax.dot_general(a, b, dims, precision=precision, preferred_element_type=F32)  6.39 us
  transfers between devices with their start and end apart: 5, of which 5 were waited for; matrix products, arithmetic and copies ran while one was open for 4% of the time, Pallas kernels for 0%

commit v1 on v0

--- a/solution.py
+++ b/solution.py
@@ -1,13 +1,20 @@
+import functools
 import math
 
 import jax
 import jax.numpy as jnp
 from jax import lax
+from jax.experimental import pallas as pl
+from jax.experimental.pallas import tpu as pltpu
 from jax.sharding import PartitionSpec as P
 
 HIGH = lax.Precision.HIGHEST
 BF = jnp.bfloat16
 F32 = jnp.float32
+Y = 8
+C = 2
+G = Y * C
+MESH = pl.DeviceIdType.MESH
 
 
 def dot(a, b, dims, precision=None):
@@ -25,23 +32,189 @@
     return dot(d, mask, (((1,), (1,)), ((), ())), HIGH)
 
 
-def three(v):
-    high = v.astype(BF)
-    rest = v - high.astype(F32)
-    mid = rest.astype(BF)
-    low = (rest - mid.astype(F32)).astype(BF)
-    return [high, mid, low]
-
-
-def chain(gain, lower):
-    n = gain.shape[0]
-    row = lax.broadcasted_iota(jnp.int32, (n, n), 0)
-    col = lax.broadcasted_iota(jnp.int32, (n, n), 1)
-    before = (col < row) if lower else (col > row)
-    terms = jnp.where(before, gain[:, None], 0.0)
-    strict = before.astype(F32)
-    total = dot(strict, terms, (((1,), (0,)), ((), ())), HIGH)
-    return jnp.where(before, jnp.exp(total), 0.0)
+def greet(peers):
+    barrier = pltpu.get_barrier_semaphore()
+    for axis, first, count, step, me in peers:
+
+        def signal(k, carry):
+            peer = first + lax.rem(me + k, count) * step
+            pl.semaphore_signal(barrier, inc=1, device_id={axis: peer}, device_id_type=MESH)
+            return carry
+
+        lax.fori_loop(1, count, signal, 0)
+    pl.semaphore_wait(barrier, sum(p[2] - 1 for p in peers))
+
+
+def spread_out(group, source, target, send_sem, recv_sem):
+    axis, first, count, step, me = group
+    pltpu.make_async_copy(source(me), target(me), recv_sem).start()
+
+    def send(k, carry):
+        peer = lax.rem(me + k, count)
+        pltpu.make_async_remote_copy(
+            src_ref=source(peer),
+            dst_ref=target(me),
+            send_sem=send_sem,
+            recv_sem=recv_sem,
+            device_id={axis: first + peer * step},
+            device_id_type=MESH,
+        ).start()
+        return carry
+
+    lax.fori_loop(1, count, send, 0)
+
+
+def take(ref, sem):
+    pltpu.make_async_copy(ref, ref, sem).wait()
+
+
+def carry_kernel(zs, f_ref, gain_ref, out_ref, held, gains, total, tgain, zheld, zgains, back, sems):
+    seq = lax.axis_index("seq")
+    z, r = seq // G, lax.rem(seq, G)
+    near = ("seq", z * G, G, 1, r)
+    far = ("seq", r, zs, G, z)
+    greet([near, far])
+    spread_out(near, lambda k: gain_ref, lambda k: gains.at[k], sems.at[0], sems.at[1])
+    spread_out(near, lambda k: f_ref.at[k], lambda k: held.at[k], sems.at[2], sems.at[3])
+    head = r // (G // 4)
+    take(gains, sems.at[1])
+    take(held, sems.at[3])
+    ups = (True, False, False, True)
+
+    def grow(ref, j, i):
+        return jnp.exp(ref[j, pl.ds((i // 2) * 4 + head, 1), :])
+
+    for i, up in enumerate(ups):
+        state = jnp.zeros(total.shape[1:], F32)
+        for j in range(G) if up else range(G - 1, -1, -1):
+            state = grow(gains, j, i) * state + held[j, i].astype(F32)
+        total[i] = state.astype(BF)
+    whole = gains[0]
+    for j in range(1, G):
+        whole = whole + gains[j]
+    tgain[...] = whole
+    spread_out(far, lambda k: tgain, lambda k: zgains.at[k], sems.at[4], sems.at[5])
+    spread_out(far, lambda k: total, lambda k: zheld.at[k], sems.at[6], sems.at[7])
+    take(zgains, sems.at[5])
+    take(zheld, sems.at[7])
+    for i, up in enumerate(ups):
+        state = jnp.zeros(total.shape[1:], F32)
+        for j in range(zs) if up else range(zs - 1, -1, -1):
+            new = grow(zgains, j, i) * state + zheld[j, i].astype(F32)
+            state = jnp.where((j < z) if up else (j > z), new, state)
+        for j in range(G) if up else range(G - 1, -1, -1):
+            back[j, i] = state.astype(BF)
+            state = grow(gains, j, i) * state + held[j, i].astype(F32)
+    spread_out(near, lambda k: back.at[k], lambda k: out_ref.at[k], sems.at[8], sems.at[9])
+    take(out_ref, sems.at[9])
+    few = G - 1
+    take(gains.at[pl.ds(0, few)], sems.at[0])
+    take(held.at[pl.ds(0, few)], sems.at[2])
+    take(zgains.at[pl.ds(0, zs - 1)], sems.at[4])
+    take(zheld.at[pl.ds(0, zs - 1)], sems.at[6])
+    take(back.at[pl.ds(0, few)], sems.at[8])
+
+
+def carry_states(f, gain, zs):
+    vmem = pl.BlockSpec(memory_space=pltpu.VMEM)
+    part = f.shape[1:]
+    return pl.pallas_call(
+        functools.partial(carry_kernel, zs),
+        out_shape=jax.ShapeDtypeStruct(f.shape, BF),
+        in_specs=[vmem, vmem],
+        out_specs=vmem,
+        scratch_shapes=[
+            pltpu.VMEM(f.shape, BF),
+            pltpu.VMEM((G,) + gain.shape, F32),
+            pltpu.VMEM(part, BF),
+            pltpu.VMEM(gain.shape, F32),
+            pltpu.VMEM((zs,) + part, BF),
+            pltpu.VMEM((zs,) + gain.shape, F32),
+            pltpu.VMEM(f.shape, BF),
+            pltpu.SemaphoreType.DMA((10,)),
+        ],
+        compiler_params=pltpu.CompilerParams(collective_id=0, has_side_effects=True),
+    )(f, gain)
+
+
+def tail_kernel(
+    zs, scale, w_ref, m_ref, f_ref, gf_ref, gw_ref, gm_ref,
+    w_core, w_mid, w_y, w_low, w_z, m_all, f_all, sems,
+):
+    seq = lax.axis_index("seq")
+    hd = lax.axis_index("head")
+    z, r = seq // G, lax.rem(seq, G)
+    y, core = r // C, lax.rem(r, C)
+    heads = m_all.shape[0]
+    along_c = ("seq", z * G + y * C, C, 1, core)
+    along_y = ("seq", z * G + core, Y, C, y)
+    along_z = ("seq", r, zs, G, z)
+    along_x = ("head", 0, heads, 1, hd)
+    greet([along_c, along_y, along_z, along_x])
+    spread_out(along_c, lambda k: w_ref.at[:, :, k], lambda k: w_core.at[k], sems.at[0], sems.at[1])
+    spread_out(along_x, lambda k: f_ref.at[k], lambda k: f_all.at[k], sems.at[2], sems.at[3])
+    spread_out(along_x, lambda k: m_ref, lambda k: m_all.at[k], sems.at[4], sems.at[5])
+    take(w_core, sems.at[1])
+    for j in range(Y):
+        w_mid[j] = (w_core[0, :, j].astype(F32) + w_core[1, :, j].astype(F32)).astype(BF)
+    spread_out(along_y, lambda k: w_mid.at[k], lambda k: w_y.at[k], sems.at[6], sems.at[7])
+    take(w_y, sems.at[7])
+    for i in range(zs):
+        low = w_y[0, i].astype(F32)
+        for j in range(1, Y):
+            low = low + w_y[j, i].astype(F32)
+        w_low[i] = low.astype(BF)
+    spread_out(along_z, lambda k: w_low.at[k], lambda k: w_z.at[k], sems.at[8], sems.at[9])
+    take(f_all, sems.at[3])
+    take(m_all, sems.at[5])
+    f = f_all[0].astype(F32)
+    for j in range(1, heads):
+        f = f + f_all[j].astype(F32)
+    gf_ref[...] = f.astype(BF)
+    n = gm_ref.shape[2]
+    for i in range(gm_ref.shape[0]):
+        m = m_all[0, :, i * n : (i + 1) * n].astype(F32)
+        for j in range(1, heads):
+            m = m + m_all[j, :, i * n : (i + 1) * n].astype(F32)
+        gm_ref[i] = m
+    take(w_z, sems.at[9])
+    low = w_z[0].astype(F32)
+    for j in range(1, zs):
+        low = low + w_z[j].astype(F32)
+    gw_ref[...] = low * scale
+    take(w_core.at[0], sems.at[0])
+    take(f_all.at[pl.ds(0, heads - 1)], sems.at[2])
+    take(m_all.at[pl.ds(0, heads - 1)], sems.at[4])
+    take(w_y.at[pl.ds(0, Y - 1)], sems.at[6])
+    take(w_z.at[pl.ds(0, zs - 1)], sems.at[8])
+
+
+def tail(w, maps, terms, zs, scale):
+    vmem = pl.BlockSpec(memory_space=pltpu.VMEM)
+    heads, frames, width = terms.shape
+    rows, cols = w.shape[3:]
+    n = maps.shape[1] // 4
+    return pl.pallas_call(
+        functools.partial(tail_kernel, zs, scale),
+        out_shape=[
+            jax.ShapeDtypeStruct((frames, width), BF),
+            jax.ShapeDtypeStruct((rows, cols), F32),
+            jax.ShapeDtypeStruct((4, frames, n), F32),
+        ],
+        in_specs=[vmem] * 3,
+        out_specs=[vmem] * 3,
+        scratch_shapes=[
+            pltpu.VMEM((C, zs, Y, rows, cols), BF),
+            pltpu.VMEM((Y, zs, rows, cols), BF),
+            pltpu.VMEM((Y, zs, rows, cols), BF),
+            pltpu.VMEM((zs, rows, cols), BF),
+            pltpu.VMEM((zs, rows, cols), BF),
+            pltpu.VMEM((heads,) + maps.shape, BF),
+            pltpu.VMEM(terms.shape, BF),
+            pltpu.SemaphoreType.DMA((10,)),
+        ],
+        compiler_params=pltpu.CompilerParams(collective_id=1, has_side_effects=True),
+    )(w, maps, terms)
 
 
 def edge(k, lower):
@@ -92,6 +265,7 @@
     heads = decay_a.shape[0]
     size = w_in.shape[1] // heads
     peers = lax.axis_size("seq")
+    heads_all = lax.axis_size("head")
     n = b_a.shape[1]
     x2 = jnp.dot(features, w_in, preferred_element_type=F32).astype(BF)
     x = x2.reshape(frames, heads, size).transpose(1, 0, 2)
@@ -100,54 +274,26 @@
     k_z = running(decay_z, False)
     wt_a, w_a, gr_a, f_a, q_a = summaries(x, g, b_a, c_a, k_a, True)
     wt_z, w_z, gr_z, f_z, q_z = summaries(x, g, b_z, c_z, k_z, False)
-    per = heads * size // peers
-    parts = [v.astype(BF).reshape(peers, per * n) for v in (f_a, q_a, f_z, q_z)]
-    gains = three(jnp.sum(decay_a, axis=1)) + three(jnp.sum(decay_z, axis=1))
-    gains = jnp.repeat(jnp.stack(gains, 1), peers // heads, axis=0)
-    gains = jnp.pad(gains, ((0, 0), (0, n - gains.shape[1])))
-    sent = jnp.concatenate(parts + [gains], axis=1)
-    got = lax.all_to_all(sent, "seq", 0, 0, tiled=True)
-    wide = per * n
-    gain = got[:, 4 * wide :].astype(F32)
-    t_a = chain(gain[:, 0] + gain[:, 1] + gain[:, 2], True)
-    t_z = chain(gain[:, 3] + gain[:, 4] + gain[:, 5], False)
-    got = got[:, : 4 * wide].astype(F32)
-    plain = (((1,), (0,)), ((), ()))
-    flip = (((0,), (0,)), ((), ()))
-    back = [
-        dot(t_a, got[:, :wide], plain, HIGH),
-        dot(t_a, got[:, wide : 2 * wide], flip, HIGH),
-        dot(t_z, got[:, 2 * wide : 3 * wide], plain, HIGH),
-        dot(t_z, got[:, 3 * wide :], flip, HIGH),
-    ]
-    back = jnp.concatenate(back, axis=1).astype(BF)
-    back = lax.all_to_all(back, "seq", 0, 0, tiled=True)
-    s_a, o_a, s_z, o_z = [
-        back[:, i * wide : (i + 1) * wide].reshape(heads, size, n) for i in range(4)
-    ]
+    rows = heads * size // G
+    sent = jnp.stack([v.astype(BF).reshape(G, rows, n) for v in (f_a, q_a, f_z, q_z)], axis=1)
+    gain = jnp.concatenate([jnp.sum(decay_a, axis=1), jnp.sum(decay_z, axis=1)])
+    gain = jnp.broadcast_to(gain[:, None], (2 * heads, n))
+    back = carry_states(sent, gain, peers // G)
+    s_a, o_a, s_z, o_z = [back[:, i].reshape(heads, size, n) for i in range(4)]
     dscores = jnp.einsum("htp,hsp->hts", g, x, preferred_element_type=F32).astype(BF).astype(F32)
     gx_a, gb_a, gc_a, gd_a = gradients(x, g, b_a, c_a, k_a, wt_a, w_a, gr_a, dscores, s_a, o_a, True)
     gx_z, gb_z, gc_z, gd_z = gradients(x, g, b_z, c_z, k_z, wt_z, w_z, gr_z, dscores, s_z, o_z, False)
     grad_x = gx_a + gx_z + skip_gain[:, None, None] * g.astype(F32)
     grad_x = grad_x.astype(BF).transpose(1, 0, 2).reshape(frames, heads * size)
     maps = jnp.concatenate([gb_a, gc_a, gb_z, gc_z], axis=1).astype(BF)
-    maps = lax.psum(maps, "head").astype(F32)
-    terms = dot(grad_x, w_in, (((1,), (1,)), ((), ()))).astype(BF)
-    grad_features = lax.psum_scatter(terms, "head", scatter_dimension=1, tiled=True)
-    weight_sum = lax.psum_scatter(
-        dot(features, grad_x, flip), "seq", scatter_dimension=0, tiled=True
+    split = w_in.reshape(heads_all, -1, w_in.shape[1])
+    terms = jnp.einsum("tk,hdk->htd", grad_x, split, preferred_element_type=F32).astype(BF)
+    weight = dot(features, grad_x, (((0,), (0,)), ((), ()))).astype(BF)
+    weight = weight.reshape(peers // G, Y, C, -1, weight.shape[1])
+    grad_features, grad_w_in, maps = tail(
+        weight, maps, terms, peers // G, 1.0 / math.sqrt(frames * peers)
     )
-    grad_w_in = weight_sum * (1.0 / math.sqrt(frames * peers))
-    return (
-        grad_features,
-        grad_w_in,
-        maps[:, :n],
-        maps[:, n : 2 * n],
-        maps[:, 2 * n : 3 * n],
-        maps[:, 3 * n :],
-        gd_a,
-        gd_z,
-    )
+    return (grad_features, grad_w_in, maps[0], maps[1], maps[2], maps[3], gd_a, gd_z)
 
 
 def solution(mesh):

time: 309 us -> 87.4 us (0.28)
  waiting for transfers between devices: 238 us -> 0 us
  Pallas kernels: 0 us -> 62 us
  starting transfers between devices: 24.1 us -> 0 us
  between operations: 15.9 us -> 0.88 us
  local copies, waits for them, and re-layouts: 14.5 us -> 11.3 us
    unnamed x4 -> x0, waiting for transfers between devices: 145 us -> none
    pallas_call x0 -> x2, Pallas kernels: none -> 62 us  [the longest x1 40.9 us: carry_states(): pl.pallas_call(functools.partial(carry_kernel, zs), out_shape=jax.ShapeDt...]
    psum x1 -> x0, waiting for transfers between devices: 35.3 us -> none  [local(): maps = lax.psum(maps, 'head').astype(F32)]
    all_to_all x2 -> x0, waiting for transfers between devices: 30 us -> none  [the longest x1 15.2 us: local(): got = lax.all_to_all(sent, 'seq', 0, 0, tiled=True)]
    reduce_scatter x1 -> x0, waiting for transfers between devices: 27.5 us -> none  [local(): lax.psum_scatter(terms, 'head', scatter_dimension=1, tiled=True)]
    all_to_all x2 -> x0, starting transfers between devices: 23.9 us -> none  [the longest x1 18.4 us: local(): got = lax.all_to_all(sent, 'seq', 0, 0, tiled=True)]
    unnamed x36 -> x27, local copies, waits for them, and re-layouts: 11.9 us -> 6.05 us
    dot_general x18 -> x11, matrix products: 6.39 us -> 4.45 us  [dot(): lax.dot_general(a, b, dims, precision=precision, preferred_element_type=F32)]
  transfers between devices with their start and end apart: 5 -> 0, of which waited for: 5 -> 0; matrix products, arithmetic and copies ran while one was open for 4% -> 0% of each run, Pallas kernels for 0% -> 0%
where the time goes in v1:
time: 87.4 us; the launch traced here: 86.6 us
  Pallas kernels  62 us (71%)
  local copies, waits for them, and re-layouts  11.3 us (13%)
  matrix products  9.71 us (11%)
  other arithmetic  2.71 us (3%)
  between operations  0.88 us (1%)
    pallas_call x1, Pallas kernels, carry_states(): pl.pallas_call(functools.partial(carry_kernel, zs), out_shape=jax.ShapeDt...  40.9 us
    pallas_call x1, Pallas kernels, tail(): pl.pallas_call(functools.partial(tail_kernel, zs, scale), out_shape=[jax....  21.1 us
    unnamed x27, local copies, waits for them, and re-layouts  6.05 us
    dot_general x11, matrix products, dot(): lax.dot_general(a, b, dims, precision=precision, preferred_element_type=F32)  4.45 us

profile of v1, /device:TPU:1, one launch (start us, length us, event | category | flops | bytes accessed | tf_op | source)
XLA Modules:
  0.0 86.6 jit_solution(12259283928040328815)
XLA Ops:
  0.7 0.9 %fusion.56 = f32[128,4]{0,1:T(4,128)S(1)} fusion(f32[4,128]{1,0:T(4,128)} %param.17), kind=kOutput, calls=%fused_computation.90 | convolution fusion | flops 802816 | bytes 4096 | tf_op jit(solution)/shard_map/dot_general | solution.py:21
  1.7 0.8 fusion.55
  2.8 1.0 %copy.59 = bf16[128,256]{0,1:T(8,128)(2,1)S(1)} copy(bf16[128,256]{1,0:T(8,128)(2,1)} %param.19) | data formatting | bytes 131072 | tf_op args[9]
  3.8 0.9 %convolution_convert_fusion.5 = bf16[4,64,128]{2,1,0:T(8,128)(2,1)S(1)} fusion(bf16[4,128,64]{1,2,0:T(8,128)(2,1)S(1)} %bitcast.166, f32[4,128]{1,0:T(4,128)S(1)} %get-tuple-element.44, bf16[128,128]{1,0:T(8,128)(2,1)} %param.13), kind=kOutput, calls=%fused_computation.20 | convolution fusion | flops 8519680 | bytes 165888 | tf_op jit(solution)/shard_map/htp,tn->hpn/dot_general | solution.py:230
  4.9 0.2 convolution_convert_fusion.7
  5.2 0.6 copy-done.3
  6.0 0.6 copy-done.6
  6.8 0.7 pad_maximum_fusion.f_ref
  7.6 0.6 copy-done.10
  8.4 0.7 broadcast_in_dim.65.gain_ref
  9.1 40.9 %shard_map.161 = bf16[16,4,16,128]{3,2,1,0:T(8,128)(2,1)} custom-call(bf16[16,4,16,128]{3,2,1,0:T(8,128)(2,1)} %pad_maximum_fusion.f_ref, f32[8,128]{1,0:T(8,128)} %broadcast_in_dim.65.gain_ref), custom_call_target="tpu_custom_call" | custom-call | tf_op jit(solution)/shard_map/pallas_call | solution.py:121
  50.0 1.0 %fusion.81 = (bf16[16,1,16,128]{3,2,1,0:T(8,128)(2,1)S(1)}, bf16[16,1,16,128]{3,2,1,0:T(8,128)(2,1)S(1)}, bf16[16,1,16,128]{3,2,1,0:T(8,128)(2,1)S(1)}, bf16[16,1,16,128]{3,2,1,0:T(8,128)(2,1)S(1)}) fusion(bf16[16,4,16,128]{3,2,1,0:T(8,128)(2,1)} %shard_map.161), kind=kLoop, calls=%fused_computation.126 | loop fusion | bytes 524288 | tf_op jit(solution)/shard_map/slice | solution.py:282
  51.1 0.3 fusion.43
  51.5 0.6 copy-done.1
  52.1 0.2 multiply_reduce_fusion.2
  52.9 0.7 copy-done.4
  53.9 0.5 fusion.25
  54.4 0.8 convolution_add_fusion.4
  56.0 0.8 convolution_add_fusion.5
  57.1 0.2 convolution_bitcast_fusion.5
  57.4 0.2 convolution_bitcast_fusion.6
  58.2 0.7 pad_maximum_fusion.1.m_ref
  59.0 0.3 fusion.4
  59.3 0.7 copy-done.11
  60.0 0.3 fusion.10
  60.3 0.3 fusion
  60.6 1.0 %copy.64 = bf16[1024,256]{1,0:T(8,128)(2,1)} copy(bf16[1024,256]{0,1:T(8,128)(2,1)S(1)} %fusion) | data formatting | bytes 1048576 | tf_op jit(solution)/shard_map/convert_element_type | solution.py:291
  61.6 1.0 %fusion.1.f_ref = bf16[4,128,256]{2,1,0:T(8,128)(2,1)} fusion(bf16[128,256,1]{0,1,2:T(8,128)(2,1)S(1)} %bitcast.190, bf16[4,256,256]{2,1,0:T(8,128)(2,1)S(1)} %bitcast.159), kind=kOutput, calls=%fused_computation.3 | convolution fusion | flops 67239936 | bytes 851968 | tf_op jit(solution)/shard_map/tk,hdk->htd/dot_general | solution.py:290
  62.6 21.1 %shard_map.162 = (bf16[128,256]{1,0:T(8,128)(2,1)}, f32[8,256]{1,0:T(8,128)}, f32[4,128,128]{2,1,0:T(8,128)}) custom-call(bf16[8,8,2,8,256]{4,3,2,1,0:T(8,128)(2,1)} %bitcast.176, bf16[128,512]{1,0:T(8,128)(2,1)} %pad_maximum_fusion.1.m_ref, bf16[4,128,256]{2,1,0:T(8,128)(2,1)} %fusion.1.f_ref), custom_call_target="tpu_custom_call" | custom-call | tf_op jit(solution)/shard_map/pallas_call | solution.py:197
  83.7 1.7 %slice_bitcast_fusion = (f32[128,128]{1,0:T(8,128)}, f32[128,128]{1,0:T(8,128)}, f32[128,128]{1,0:T(8,128)}, f32[128,128]{1,0:T(8,128)}) fusion(f32[4,128,128]{2,1,0:T(8,128)} %get-tuple-element.13), kind=kLoop, calls=%fused_computation.83 | loop fusion | bytes 524288 | tf_op jit(solution)/shard_map/squeeze | solution.py:296
  85.3 0.6 copy.98
  86.0 0.6 copy.99
  (52 shorter events, 4.5 us)
Async XLA Ops:
  0.6 4.2 %copy-start = (bf16[1024,256]{1,0:T(8,128)(2,1)S(1)}, bf16[1024,256]{1,0:T(8,128)(2,1)}, u32[]{:S(2)}) copy-start(bf16[1024,256]{1,0:T(8,128)(2,1)} %param.11) | copy-start | bytes 1572868
  0.6 4.2 %copy-start.2 = (bf16[128,1024]{1,0:T(8,128)(2,1)S(1)}, bf16[128,1024]{1,0:T(8,128)(2,1)}, u32[]{:S(2)}) copy-start(bf16[128,1024]{1,0:T(8,128)(2,1)} %param.10) | copy-start | bytes 786436
  3.7 0.9 %copy-start.5 = (bf16[128,128]{1,0:T(8,128)(2,1)S(1)}, bf16[128,128]{1,0:T(8,128)(2,1)}, u32[]{:S(2)}) copy-start(bf16[128,128]{1,0:T(8,128)(2,1)} %param.15) | copy-start | bytes 98308
  5.1 0.8 copy-start.3
  5.9 0.8 copy-start.6
  6.8 0.7 copy-start.9
  7.5 0.7 copy-start.10
  51.1 1.0 %copy-start.1 = (bf16[16,4,16,128]{3,2,1,0:T(8,128)(2,1)S(1)}, bf16[16,4,16,128]{3,2,1,0:T(8,128)(2,1)}, u32[]{:S(2)}) copy-start(bf16[16,4,16,128]{3,2,1,0:T(8,128)(2,1)} %shard_map.161) | copy-start | bytes 786436
  52.9 0.8 copy-start.4
  59.3 0.7 copy-start.11
  83.7 1.7 %copy-start.7 = (bf16[128,256]{1,0:T(8,128)(2,1)S(1)}, bf16[128,256]{1,0:T(8,128)(2,1)}, u32[]{:S(2)}) copy-start(bf16[128,256]{1,0:T(8,128)(2,1)} %get-tuple-element.56) | copy-start | bytes 196612
  85.3 0.7 copy-start.8

commit v2 on v0

v2 whole, which is shorter than its diff:
```python
import functools
import math

import jax
import jax.numpy as jnp
from jax import lax
from jax.experimental import pallas as pl
from jax.experimental.pallas import tpu as pltpu
from jax.sharding import PartitionSpec as P

HIGH = lax.Precision.HIGHEST
BF = jnp.bfloat16
F32 = jnp.float32
Y = 8
C = 2
G = Y * C
MESH = pl.DeviceIdType.MESH


def greet(peers):
    barrier = pltpu.get_barrier_semaphore()
    for axis, first, count, step, me in peers:

        def signal(k, carry):
            peer = first + lax.rem(me + k, count) * step
            pl.semaphore_signal(barrier, inc=1, device_id={axis: peer}, device_id_type=MESH)
            return carry

        lax.fori_loop(1, count, signal, 0)


def greeted(peers):
    pl.semaphore_wait(pltpu.get_barrier_semaphore(), sum(p[2] - 1 for p in peers))


def spread_out(group, source, target, send_sem, recv_sem):
    axis, first, count, step, me = group
    pltpu.make_async_copy(source(me), target(me), recv_sem).start()

    def send(k, carry):
        peer = lax.rem(me + k, count)
        pltpu.make_async_remote_copy(
            src_ref=source(peer),
            dst_ref=target(me),
            send_sem=send_sem,
            recv_sem=recv_sem,
            device_id={axis: first + peer * step},
            device_id_type=MESH,
        ).start()
        return carry

    lax.fori_loop(1, count, send, 0)


def take(ref, sem):
    pltpu.make_async_copy(ref, ref, sem).wait()


NN = (((1,), (0,)), ((), ()))
NT = (((1,), (1,)), ((), ()))
TN = (((0,), (0,)), ((), ()))
UPS = ((True, False), (False, True))


def dot(a, b, dims, precision=None):
    return lax.dot_general(a, b, dims, precision=precision, preferred_element_type=F32)


def iota(shape, axis):
    return lax.broadcasted_iota(jnp.int32, shape, axis)


def layer_kernel(
    zs, heads, scale,
    x_ref, w_ref, ba_ref, ca_ref, bz_ref, cz_ref, da_ref, dz_ref, skip_ref, g_ref,
    gf_ref, gw_ref, gba_ref, gca_ref, gbz_ref, gcz_ref, gda_ref, gdz_ref,
    d8, sent, held, gains, total, tgain, zheld, zgains, back, states, ds,
    w_all, w_core, w_mid, w_y, w_low, w_z, m_own, m_all, f_own, f_all, sems,
):
    seq = lax.axis_index("seq")
    hd = lax.axis_index("head")
    z, r = seq // G, lax.rem(seq, G)
    y, core = r // C, lax.rem(r, C)
    groups = f_all.shape[0]
    near = ("seq", z * G, G, 1, r)
    far = ("seq", r, zs, G, z)
    along_c = ("seq", z * G + y * C, C, 1, core)
    along_y = ("seq", z * G + core, Y, C, y)
    along_x = ("head", 0, groups, 1, hd)
    greet([near, far, along_x])

    frames, wide = g_ref.shape
    size = wide // heads
    n = ba_ref.shape[1]
    rows = wide // G
    low_mask = iota((frames, frames), 1) <= iota((frames, frames), 0)
    high_mask = iota((frames, frames), 1) >= iota((frames, frames), 0)
    low_f, high_f = low_mask.astype(F32), high_mask.astype(F32)
    which = iota((2 * heads, wide), 1) // size
    pick = [(iota((2 * heads, wide), 0) - i * heads == which).astype(F32) for i in range(2)]
    d8[0:heads, :] = da_ref[...]
    d8[heads : 2 * heads, :] = dz_ref[...]
    d = d8[...]
    tgain[0] = jnp.broadcast_to(jnp.sum(d, axis=1, keepdims=True), (2 * heads, n))
    k_row = [dot(d, low_f, NT, HIGH), dot(d, high_f, NT, HIGH)]
    k_all = [dot(k_row[i], pick[i], TN, HIGH) for i in range(2)]
    edge = [k_all[0][frames - 1 : frames], k_all[1][0:1]]
    weight = [jnp.exp(edge[i] - k_all[i]) for i in range(2)]
    growth = [jnp.exp(k_all[i]) for i in range(2)]
    g = g_ref[...]
    g32 = g.astype(F32)
    grown = [(g32 * growth[i]).astype(BF) for i in range(2)]
    maps_b = [ba_ref, bz_ref]
    maps_c = [ca_ref, cz_ref]
    x = dot(x_ref[...], w_ref[...], NN).astype(BF)
    x32 = x.astype(F32)
    weighted = [(x32 * weight[i]).astype(BF) for i in range(2)]
    greeted([near, far, along_x])
    spread_out(near, lambda k: tgain.at[0], lambda k: gains.at[k], sems.at[0], sems.at[1])
    for i in range(2):
        fresh = dot(weighted[i], maps_b[i][...], TN).astype(BF)
        query = dot(grown[i], maps_c[i][...], TN).astype(BF)
        sent[i, :, 0] = fresh.reshape(G, rows, n)
        sent[i, :, 1] = query.reshape(G, rows, n)
        spread_out(
            near, lambda k: sent.at[i, k], lambda k: held.at[i, k], sems.at[2 + i], sems.at[4 + i]
        )

    lane_head = iota((frames, wide), 1) // size
    grad_x = jnp.zeros((frames, wide), F32)
    dk = jnp.zeros((2 * heads, frames), F32)
    daff = [None, None]
    for i in range(2):
        mask = low_mask if i == 0 else high_mask
        aff = dot(maps_c[i][...], maps_b[i][...], NT)
        pull = jnp.zeros((frames, frames), F32)
        for h in range(heads):
            gm = jnp.where(lane_head == h, g32, 0.0).astype(BF)
            if i == 0:
                ds[h] = dot(gm, x, NT).astype(BF)
            dscores = ds[h].astype(F32)
            row = i * heads + h
            kc = k_all[i][:, h * size : h * size + 1]
            kr = k_row[i][row : row + 1]
            decays = jnp.where(mask, jnp.exp(jnp.where(mask, kc - kr, 0.0)), 0.0)
            scores = decays * aff
            grad_x = grad_x + dot(scores.astype(BF), gm, TN)
            pull = pull + dscores * decays
            e = dscores * scores
            mine = iota((2 * heads, frames), 0) == row
            dk = dk + dot(mine.astype(F32), e, NT, HIGH)
            dk = dk - jnp.where(mine, jnp.sum(e, axis=0, keepdims=True), 0.0)
        daff[i] = pull.astype(BF)
        if i == 0:
            take(gains, sems.at[1])
            head = r // (G // heads)

            def grow(ref, j, side):
                return jnp.exp(ref[j, pl.ds(side * heads + head, 1), :])

            whole = gains[0]
            for j in range(1, G):
                whole = whole + gains[j]
            tgain[1] = whole
            spread_out(far, lambda k: tgain.at[1], lambda k: zgains.at[k], sems.at[6], sems.at[7])
            for side in range(2):
                take(held.at[side], sems.at[4 + side])
                for j0, up in enumerate(UPS[side]):
                    state = jnp.zeros((rows, n), F32)
                    for j in range(G) if up else range(G - 1, -1, -1):
                        state = grow(gains, j, side) * state + held[side, j, j0].astype(F32)
                    total[side, j0] = state.astype(BF)
                spread_out(
                    far,
                    lambda k: total.at[side],
                    lambda k: zheld.at[side, k],
                    sems.at[8 + side],
                    sems.at[10 + side],
                )

    take(zgains, sems.at[7])
    for side in range(2):
        take(zheld.at[side], sems.at[10 + side])
        for j0, up in enumerate(UPS[side]):
            state = jnp.zeros((rows, n), F32)
            for j in range(zs) if up else range(zs - 1, -1, -1):
                new = grow(zgains, j, side) * state + zheld[side, j, j0].astype(F32)
                state = jnp.where((j < z) if up else (j > z), new, state)
            for j in range(G) if up else range(G - 1, -1, -1):
                back[side, j, j0] = state.astype(BF)
                state = grow(gains, j, side) * state + held[side, j, j0].astype(F32)
        spread_out(
            near,
            lambda k: back.at[side, k],
            lambda k: states.at[side, k],
            sems.at[12 + side],
            sems.at[14 + side],
        )
    grad_b = [dot(daff[i], maps_c[i][...], TN) for i in range(2)]
    grad_c = [dot(daff[i], maps_b[i][...], NN) for i in range(2)]
    lane = iota((1, wide), 1) // size
    skip = jnp.zeros((1, wide), F32)
    for h in range(heads):
        skip = jnp.where(lane == h, skip_ref[h], skip)
    grad_x = grad_x + skip * g32

    last = jnp.zeros((2 * heads, n), F32)
    for i in range(2):
        take(states.at[i], sems.at[14 + i])
        s_in = states[i, :, 0].reshape(wide, n)
        g_out = states[i, :, 1].reshape(wide, n)
        scaled = dot(maps_b[i][...], g_out, NT) * weight[i]
        grad_x = grad_x + scaled
        u = dot(pick[i], scaled * x32, NT, HIGH)
        carried = dot(maps_c[i][...], s_in, NT) * growth[i] * g32
        dk = dk - u + dot(pick[i], carried, NT, HIGH)
        both = dot(pick[i], g_out.astype(F32) * s_in.astype(F32), NN, HIGH)
        fall = jnp.exp(jnp.sum(d, axis=1, keepdims=True))
        last = last + u + fall * both
        m_own[:, (2 * i) * n : (2 * i + 1) * n] = (grad_b[i] + dot(weighted[i], g_out, NN)).astype(BF)
        m_own[:, (2 * i + 1) * n : (2 * i + 2) * n] = (grad_c[i] + dot(grown[i], s_in, NN)).astype(BF)
    gx = grad_x.astype(BF)
    piece = Y * C * w_all.shape[3]
    for k in range(zs):
        part = dot(x_ref[:, k * piece : (k + 1) * piece], gx, TN)
        w_all[k] = part.reshape(w_all.shape[1:]).astype(BF)
    spread_out(along_c, lambda k: w_all.at[:, :, k], lambda k: w_core.at[k], sems.at[16], sems.at[17])
    spread_out(along_x, lambda k: m_own, lambda k: m_all.at[k], sems.at[18], sems.at[19])
    for k in range(groups):
        f_own[k] = dot(gx, w_ref[k * wide : (k + 1) * wide, :], NT).astype(BF)
    spread_out(along_x, lambda k: f_own.at[k], lambda k: f_all.at[k], sems.at[20], sems.at[21])
    tri = jnp.where(iota((2 * heads, frames), 0) < heads, dot(dk, low_f, NN, HIGH), dot(dk, high_f, NN, HIGH))
    grad_d = tri + jnp.sum(last, axis=1, keepdims=True)
    gda_ref[...] = grad_d[0:heads]
    gdz_ref[...] = grad_d[heads : 2 * heads]
    take(w_core, sems.at[17])
    for j in range(Y):
        w_mid[j] = (w_core[0, :, j].astype(F32) + w_core[1, :, j].astype(F32)).astype(BF)
    spread_out(along_y, lambda k: w_mid.at[k], lambda k: w_y.at[k], sems.at[22], sems.at[23])
    take(w_y, sems.at[23])
    for i in range(zs):
        low = w_y[0, i].astype(F32)
        for j in range(1, Y):
            low = low + w_y[j, i].astype(F32)
        w_low[i] = low.astype(BF)
    spread_out(far, lambda k: w_low.at[k], lambda k: w_z.at[k], sems.at[24], sems.at[25])
    take(m_all, sems.at[19])
    for i, ref in enumerate((gba_ref, gca_ref, gbz_ref, gcz_ref)):
        m = m_all[0, :, i * n : (i + 1) * n].astype(F32)
        for j in range(1, groups):
            m = m + m_all[j, :, i * n : (i + 1) * n].astype(F32)
        ref[...] = m
    take(f_all, sems.at[21])
    f = f_all[0].astype(F32)
    for j in range(1, groups):
        f = f + f_all[j].astype(F32)
    gf_ref[...] = f.astype(BF)
    take(w_z, sems.at[25])
    low = w_z[0].astype(F32)
    for j in range(1, zs):
        low = low + w_z[j].astype(F32)
    gw_ref[...] = low * scale
    few, far_few, x_few = pl.ds(0, G - 1), pl.ds(0, zs - 1), pl.ds(0, groups - 1)
    take(gains.at[few], sems.at[0])
    take(zgains.at[far_few], sems.at[6])
    for i in range(2):
        take(held.at[i, few], sems.at[2 + i])
        take(zheld.at[i, far_few], sems.at[8 + i])
        take(back.at[i, few], sems.at[12 + i])
    take(w_core.at[0], sems.at[16])
    take(m_all.at[x_few], sems.at[18])
    take(f_all.at[x_few], sems.at[20])
    take(w_y.at[pl.ds(0, Y - 1)], sems.at[22])
    take(w_z.at[far_few], sems.at[24])


def local(*args):
    features, w_in, b_a, _, _, _, decay_a, _, _, grad_y = args
    frames, deep = features.shape
    heads = decay_a.shape[0]
    wide = w_in.shape[1]
    n = b_a.shape[1]
    zs = lax.axis_size("seq") // G
    groups = lax.axis_size("head")
    cut = deep // (zs * G)
    rows = wide // G
    vmem = pl.BlockSpec(memory_space=pltpu.VMEM)
    smem = pl.BlockSpec(memory_space=pltpu.SMEM)
    scale = 1.0 / math.sqrt(frames * zs * G)
    out = jax.ShapeDtypeStruct
    return pl.pallas_call(
        functools.partial(layer_kernel, zs, heads, scale),
        out_shape=[
            out((frames, deep // groups), BF),
            out((cut, wide), F32),
            out((frames, n), F32),
            out((frames, n), F32),
            out((frames, n), F32),
            out((frames, n), F32),
            out((heads, frames), F32),
            out((heads, frames), F32),
        ],
        in_specs=[vmem] * 8 + [smem, vmem],
        out_specs=[vmem] * 8,
        scratch_shapes=[
            pltpu.VMEM((2 * heads, frames), F32),
            pltpu.VMEM((2, G, 2, rows, n), BF),
            pltpu.VMEM((2, G, 2, rows, n), BF),
            pltpu.VMEM((G, 2 * heads, n), F32),
            pltpu.VMEM((2, 2, rows, n), BF),
            pltpu.VMEM((2, 2 * heads, n), F32),
            pltpu.VMEM((2, zs, 2, rows, n), BF),
            pltpu.VMEM((zs, 2 * heads, n), F32),
            pltpu.VMEM((2, G, 2, rows, n), BF),
            pltpu.VMEM((2, G, 2, rows, n), BF),
            pltpu.VMEM((heads, frames, frames), BF),
            pltpu.VMEM((zs, Y, C, cut, wide), BF),
            pltpu.VMEM((C, zs, Y, cut, wide), BF),
            pltpu.VMEM((Y, zs, cut, wide), BF),
            pltpu.VMEM((Y, zs, cut, wide), BF),
            pltpu.VMEM((zs, cut, wide), BF),
            pltpu.VMEM((zs, cut, wide), BF),
            pltpu.VMEM((frames, 4 * n), BF),
            pltpu.VMEM((groups, frames, 4 * n), BF),
            pltpu.VMEM((groups, frames, wide), BF),
            pltpu.VMEM((groups, frames, wide), BF),
            pltpu.SemaphoreType.DMA((26,)),
        ],
        compiler_params=pltpu.CompilerParams(collective_id=0, has_side_effects=True),
    )(*args)


def solution(mesh):
    in_specs = (
        P("seq", None),
        P(None, "head"),
        P("seq", None),
        P("seq", None),
        P("seq", None),
        P("seq", None),
        P("head", "seq"),
        P("head", "seq"),
        P("head"),
        P("seq", "head"),
    )
    out_specs = (
        P("seq", "head"),
        P("seq", "head"),
        P("seq", None),
        P("seq", None),
        P("seq", None),
        P("seq", None),
        P("head", "seq"),
        P("head", "seq"),
    )
    return jax.shard_map(local, mesh=mesh, in_specs=in_specs, out_specs=out_specs, check_vma=False)
```

time: 309 us -> 62 us (0.20)
  waiting for transfers between devices: 238 us -> 0 us
  Pallas kernels: 0 us -> 54.3 us
  starting transfers between devices: 24.1 us -> 0 us
  between operations: 15.9 us -> 0.67 us
  matrix products: 9.98 us -> 0 us
  local copies, waits for them, and re-layouts: 14.5 us -> 6.62 us
  other arithmetic: 4.28 us -> 0 us
    unnamed x4 -> x0, waiting for transfers between devices: 145 us -> none
    pallas_call x0 -> x1, Pallas kernels: none -> 54.3 us  [local(): pl.pallas_call(functools.partial(layer_kernel, zs, heads, scale), out_sha...]
    psum x1 -> x0, waiting for transfers between devices: 35.3 us -> none  [local(): maps = lax.psum(maps, 'head').astype(F32)]
    all_to_all x2 -> x0, waiting for transfers between devices: 30 us -> none  [the longest x1 15.2 us: local(): got = lax.all_to_all(sent, 'seq', 0, 0, tiled=True)]
    reduce_scatter x1 -> x0, waiting for transfers between devices: 27.5 us -> none  [local(): lax.psum_scatter(terms, 'head', scatter_dimension=1, tiled=True)]
    all_to_all x2 -> x0, starting transfers between devices: 23.9 us -> none  [the longest x1 18.4 us: local(): got = lax.all_to_all(sent, 'seq', 0, 0, tiled=True)]
    dot_general x34 -> x0, matrix products: 9.98 us -> none  [the longest x18 6.39 us: dot(): lax.dot_general(a, b, dims, precision=precision, preferred_element_type=F32)]
    unnamed x36 -> x22, local copies, waits for them, and re-layouts: 11.9 us -> 6.62 us
  transfers between devices with their start and end apart: 5 -> 0, of which waited for: 5 -> 0; matrix products, arithmetic and copies ran while one was open for 4% -> 0% of each run, Pallas kernels for 0% -> 0%
where the time goes in v2:
time: 62 us; the launch traced here: 61.6 us
  Pallas kernels  54.3 us (88%)
  local copies, waits for them, and re-layouts  6.62 us (11%)
  between operations  0.67 us (1%)
    pallas_call x1, Pallas kernels, local(): pl.pallas_call(functools.partial(layer_kernel, zs, heads, scale), out_sha...  54.3 us
    unnamed x22, local copies, waits for them, and re-layouts  6.62 us

profile of v2, /device:TPU:1, one launch (start us, length us, event | category | flops | bytes accessed | tf_op | source)
XLA Modules:
  0.0 61.6 jit_solution(6433589311147065798)
XLA Ops:
  0.6 54.3 %shard_map.161 = (bf16[128,256]{1,0:T(8,128)(2,1)}, f32[8,256]{1,0:T(8,128)}, f32[128,128]{1,0:T(8,128)}, f32[128,128]{1,0:T(8,128)}, f32[128,128]{1,0:T(8,128)}...) custom-call(bf16[128,1024]{1,0:T(8,128)(2,1)} %x_ref.1, bf16[1024,256]{1,0:T(8,128)(2,1)} %w_ref.1, ...), custom_call_target="tpu_custom_call" | custom-call | tf_op jit(solution)/shard_map/pallas_call | solution.py:291
  55.0 0.0 copy-start.4
  55.0 0.0 copy-start.3
  55.0 1.5 %copy.26 = bf16[128,256]{1,0:T(8,128)(2,1)} copy(bf16[128,256]{1,0:T(8,128)(2,1)} %get-tuple-element.16) | data formatting | bytes 131072
  56.5 0.0 copy-done.4
  56.5 0.6 copy.27
  57.1 0.0 copy-done.3
  57.1 0.0 copy-start.2
  57.1 0.6 %copy.28 = f32[128,128]{1,0:T(8,128)} copy(f32[128,128]{1,0:T(8,128)S(1)} %copy-done.3) | data formatting | bytes 131072
  57.8 0.2 copy-done.2
  58.0 0.0 copy-start.1
  58.0 0.6 %copy.29 = f32[128,128]{1,0:T(8,128)} copy(f32[128,128]{1,0:T(8,128)S(1)} %copy-done.2) | data formatting | bytes 131072
  58.6 0.2 copy-done.1
  58.8 0.0 copy-start
  58.8 0.6 %copy.30 = f32[128,128]{1,0:T(8,128)} copy(f32[128,128]{1,0:T(8,128)S(1)} %copy-done.1) | data formatting | bytes 131072
  59.5 0.2 copy-done
  59.7 0.0 copy-start.6
  59.7 0.6 %copy.31 = f32[128,128]{1,0:T(8,128)} copy(f32[128,128]{1,0:T(8,128)S(1)} %copy-done) | data formatting | bytes 131072
  60.3 0.0 copy-done.6
  60.4 0.0 copy-start.5
  60.4 0.6 copy.32
  61.0 0.1 copy-done.5
  61.1 0.6 copy.33
Async XLA Ops:
  55.0 1.5 %copy-start.4 = (f32[8,256]{1,0:T(8,128)S(1)}, f32[8,256]{1,0:T(8,128)}, u32[]{:S(2)}) copy-start(f32[8,256]{1,0:T(8,128)} %get-tuple-element.17) | copy-start | bytes 24580
  55.0 2.1 %copy-start.3 = (f32[128,128]{1,0:T(8,128)S(1)}, f32[128,128]{1,0:T(8,128)}, u32[]{:S(2)}) copy-start(f32[128,128]{1,0:T(8,128)} %get-tuple-element.18) | copy-start | bytes 196612
  57.1 0.9 %copy-start.2 = (f32[128,128]{1,0:T(8,128)S(1)}, f32[128,128]{1,0:T(8,128)}, u32[]{:S(2)}) copy-start(f32[128,128]{1,0:T(8,128)} %get-tuple-element.19) | copy-start | bytes 196612
  58.0 0.9 %copy-start.1 = (f32[128,128]{1,0:T(8,128)S(1)}, f32[128,128]{1,0:T(8,128)}, u32[]{:S(2)}) copy-start(f32[128,128]{1,0:T(8,128)} %get-tuple-element.20) | copy-start | bytes 196612
  58.8 0.9 %copy-start = (f32[128,128]{1,0:T(8,128)S(1)}, f32[128,128]{1,0:T(8,128)}, u32[]{:S(2)}) copy-start(f32[128,128]{1,0:T(8,128)} %get-tuple-element.21) | copy-start | bytes 196612
  59.7 0.7 %copy-start.6 = (f32[4,128]{1,0:T(4,128)S(1)}, f32[4,128]{1,0:T(4,128)}, u32[]{:S(2)}) copy-start(f32[4,128]{1,0:T(4,128)} %get-tuple-element.22) | copy-start | bytes 6148
  60.4 0.7 %copy-start.5 = (f32[4,128]{1,0:T(4,128)S(1)}, f32[4,128]{1,0:T(4,128)}, u32[]{:S(2)}) copy-start(f32[4,128]{1,0:T(4,128)} %get-tuple-element.23) | copy-start | bytes 6148

commit v3 on v2

--- a/solution.py
+++ b/solution.py
@@ -75,7 +75,7 @@
     x_ref, w_ref, ba_ref, ca_ref, bz_ref, cz_ref, da_ref, dz_ref, skip_ref, g_ref,
     gf_ref, gw_ref, gba_ref, gca_ref, gbz_ref, gcz_ref, gda_ref, gdz_ref,
     d8, sent, held, gains, total, tgain, zheld, zgains, back, states, ds,
-    w_all, w_core, w_mid, w_y, w_low, w_z, m_own, m_all, f_own, f_all, sems,
+    w_all, w_core, w_mid, w_one, w_low, w_two, m_own, m_all, f_own, f_all, sems,
 ):
     seq = lax.axis_index("seq")
     hd = lax.axis_index("head")
@@ -109,7 +109,6 @@
     growth = [jnp.exp(k_all[i]) for i in range(2)]
     g = g_ref[...]
     g32 = g.astype(F32)
-    grown = [(g32 * growth[i]).astype(BF) for i in range(2)]
     maps_b = [ba_ref, bz_ref]
     maps_c = [ca_ref, cz_ref]
     x = dot(x_ref[...], w_ref[...], NN).astype(BF)
@@ -119,7 +118,7 @@
     spread_out(near, lambda k: tgain.at[0], lambda k: gains.at[k], sems.at[0], sems.at[1])
     for i in range(2):
         fresh = dot(weighted[i], maps_b[i][...], TN).astype(BF)
-        query = dot(grown[i], maps_c[i][...], TN).astype(BF)
+        query = dot(g32 * growth[i], maps_c[i][...].astype(F32), TN, HIGH).astype(BF)
         sent[i, :, 0] = fresh.reshape(G, rows, n)
         sent[i, :, 1] = query.reshape(G, rows, n)
         spread_out(
@@ -169,7 +168,7 @@
                     state = jnp.zeros((rows, n), F32)
                     for j in range(G) if up else range(G - 1, -1, -1):
                         state = grow(gains, j, side) * state + held[side, j, j0].astype(F32)
-                    total[side, j0] = state.astype(BF)
+                    total[side, j0] = state
                 spread_out(
                     far,
                     lambda k: total.at[side],
@@ -184,10 +183,10 @@
         for j0, up in enumerate(UPS[side]):
             state = jnp.zeros((rows, n), F32)
             for j in range(zs) if up else range(zs - 1, -1, -1):
-                new = grow(zgains, j, side) * state + zheld[side, j, j0].astype(F32)
+                new = grow(zgains, j, side) * state + zheld[side, j, j0]
                 state = jnp.where((j < z) if up else (j > z), new, state)
             for j in range(G) if up else range(G - 1, -1, -1):
-                back[side, j, j0] = state.astype(BF)
+                back[side, j, j0] = state
                 state = grow(gains, j, side) * state + held[side, j, j0].astype(F32)
         spread_out(
             near,
@@ -209,22 +208,31 @@
         take(states.at[i], sems.at[14 + i])
         s_in = states[i, :, 0].reshape(wide, n)
         g_out = states[i, :, 1].reshape(wide, n)
-        scaled = dot(maps_b[i][...], g_out, NT) * weight[i]
+        g_low = g_out.astype(BF)
+        scaled = dot(maps_b[i][...], g_low, NT) * weight[i]
         grad_x = grad_x + scaled
         u = dot(pick[i], scaled * x32, NT, HIGH)
-        carried = dot(maps_c[i][...], s_in, NT) * growth[i] * g32
+        carried = dot(maps_c[i][...].astype(F32), s_in, NT, HIGH) * growth[i] * g32
         dk = dk - u + dot(pick[i], carried, NT, HIGH)
-        both = dot(pick[i], g_out.astype(F32) * s_in.astype(F32), NN, HIGH)
+        both = dot(pick[i], g_out * s_in, NN, HIGH)
         fall = jnp.exp(jnp.sum(d, axis=1, keepdims=True))
         last = last + u + fall * both
-        m_own[:, (2 * i) * n : (2 * i + 1) * n] = (grad_b[i] + dot(weighted[i], g_out, NN)).astype(BF)
-        m_own[:, (2 * i + 1) * n : (2 * i + 2) * n] = (grad_c[i] + dot(grown[i], s_in, NN)).astype(BF)
+        m_own[:, (2 * i) * n : (2 * i + 1) * n] = (grad_b[i] + dot(weighted[i], g_low, NN)).astype(BF)
+        m_own[:, (2 * i + 1) * n : (2 * i + 2) * n] = (grad_c[i] + dot(g32 * growth[i], s_in, NN, HIGH)).astype(BF)
     gx = grad_x.astype(BF)
-    piece = Y * C * w_all.shape[3]
+    piece = Y * C * w_all.shape[4]
     for k in range(zs):
         part = dot(x_ref[:, k * piece : (k + 1) * piece], gx, TN)
-        w_all[k] = part.reshape(w_all.shape[1:]).astype(BF)
-    spread_out(along_c, lambda k: w_all.at[:, :, k], lambda k: w_core.at[k], sems.at[16], sems.at[17])
+        for i in range(2):
+            w_all[i, k] = part[:, i * n : (i + 1) * n].reshape(w_all.shape[2:]).astype(BF)
+    for i in range(2):
+        spread_out(
+            along_c,
+            lambda k: w_all.at[i, :, :, k],
+            lambda k: w_core.at[i, k],
+            sems.at[16 + i],
+            sems.at[26 + i],
+        )
     spread_out(along_x, lambda k: m_own, lambda k: m_all.at[k], sems.at[18], sems.at[19])
     for k in range(groups):
         f_own[k] = dot(gx, w_ref[k * wide : (k + 1) * wide, :], NT).astype(BF)
@@ -233,17 +241,35 @@
     grad_d = tri + jnp.sum(last, axis=1, keepdims=True)
     gda_ref[...] = grad_d[0:heads]
     gdz_ref[...] = grad_d[heads : 2 * heads]
-    take(w_core, sems.at[17])
-    for j in range(Y):
-        w_mid[j] = (w_core[0, :, j].astype(F32) + w_core[1, :, j].astype(F32)).astype(BF)
-    spread_out(along_y, lambda k: w_mid.at[k], lambda k: w_y.at[k], sems.at[22], sems.at[23])
-    take(w_y, sems.at[23])
-    for i in range(zs):
-        low = w_y[0, i].astype(F32)
-        for j in range(1, Y):
-            low = low + w_y[j, i].astype(F32)
-        w_low[i] = low.astype(BF)
-    spread_out(far, lambda k: w_low.at[k], lambda k: w_z.at[k], sems.at[24], sems.at[25])
+    first, second = (along_y, far), (far, along_y)
+    for i in range(2):
+        take(w_core.at[i], sems.at[26 + i])
+        for j in range(Y):
+            if i == 0:
+                w_mid[i, j] = (w_core[i, 0, :, j].astype(F32) + w_core[i, 1, :, j].astype(F32)).astype(BF)
+            else:
+                w_mid[i, j] = (w_core[i, 0, j].astype(F32) + w_core[i, 1, j].astype(F32)).astype(BF)
+        spread_out(
+            first[i],
+            lambda k: w_mid.at[i, k],
+            lambda k: w_one.at[i, k],
+            sems.at[22 + i],
+            sems.at[28 + i],
+        )
+    for i in range(2):
+        take(w_one.at[i], sems.at[28 + i])
+        for k in range(Y):
+            low = w_one[i, 0, k].astype(F32)
+            for j in range(1, Y):
+                low = low + w_one[i, j, k].astype(F32)
+            w_low[i, k] = low.astype(BF)
+        spread_out(
+            second[i],
+            lambda k: w_low.at[i, k],
+            lambda k: w_two.at[i, k],
+            sems.at[24 + i],
+            sems.at[30 + i],
+        )
     take(m_all, sems.at[19])
     for i, ref in enumerate((gba_ref, gca_ref, gbz_ref, gcz_ref)):
         m = m_all[0, :, i * n : (i + 1) * n].astype(F32)
@@ -255,11 +281,12 @@
     for j in range(1, groups):
         f = f + f_all[j].astype(F32)
     gf_ref[...] = f.astype(BF)
-    take(w_z, sems.at[25])
-    low = w_z[0].astype(F32)
-    for j in range(1, zs):
-        low = low + w_z[j].astype(F32)
-    gw_ref[...] = low * scale
+    for i in range(2):
+        take(w_two.at[i], sems.at[30 + i])
+        low = w_two[i, 0].astype(F32)
+        for j in range(1, Y):
+            low = low + w_two[i, j].astype(F32)
+        gw_ref[:, i * n : (i + 1) * n] = low * scale
     few, far_few, x_few = pl.ds(0, G - 1), pl.ds(0, zs - 1), pl.ds(0, groups - 1)
     take(gains.at[few], sems.at[0])
     take(zgains.at[far_few], sems.at[6])
@@ -267,11 +294,17 @@
         take(held.at[i, few], sems.at[2 + i])
         take(zheld.at[i, far_few], sems.at[8 + i])
         take(back.at[i, few], sems.at[12 + i])
-    take(w_core.at[0], sems.at[16])
     take(m_all.at[x_few], sems.at[18])
     take(f_all.at[x_few], sems.at[20])
-    take(w_y.at[pl.ds(0, Y - 1)], sems.at[22])
-    take(w_z.at[far_few], sems.at[24])
+    for i in range(2):
+        take(w_core.at[i, 0], sems.at[16 + i])
+        take(w_one.at[i, far_few], sems.at[22 + i])
+        take(w_two.at[i, far_few], sems.at[24 + i])
+
+
+def hand_over(*refs):
+    for source, target in zip(refs[:8], refs[8:]):
+        target[...] = source[...]
 
 
 def local(*args):
@@ -288,18 +321,19 @@
     smem = pl.BlockSpec(memory_space=pltpu.SMEM)
     scale = 1.0 / math.sqrt(frames * zs * G)
     out = jax.ShapeDtypeStruct
-    return pl.pallas_call(
+    shapes = [
+        out((frames, deep // groups), BF),
+        out((cut, wide), F32),
+        out((frames, n), F32),
+        out((frames, n), F32),
+        out((frames, n), F32),
+        out((frames, n), F32),
+        out((heads, frames), F32),
+        out((heads, frames), F32),
+    ]
+    results = pl.pallas_call(
         functools.partial(layer_kernel, zs, heads, scale),
-        out_shape=[
-            out((frames, deep // groups), BF),
-            out((cut, wide), F32),
-            out((frames, n), F32),
-            out((frames, n), F32),
-            out((frames, n), F32),
-            out((frames, n), F32),
-            out((heads, frames), F32),
-            out((heads, frames), F32),
-        ],
+        out_shape=shapes,
         in_specs=[vmem] * 8 + [smem, vmem],
         out_specs=[vmem] * 8,
         scratch_shapes=[
@@ -307,27 +341,30 @@
             pltpu.VMEM((2, G, 2, rows, n), BF),
             pltpu.VMEM((2, G, 2, rows, n), BF),
             pltpu.VMEM((G, 2 * heads, n), F32),
-            pltpu.VMEM((2, 2, rows, n), BF),
+            pltpu.VMEM((2, 2, rows, n), F32),
             pltpu.VMEM((2, 2 * heads, n), F32),
-            pltpu.VMEM((2, zs, 2, rows, n), BF),
+            pltpu.VMEM((2, zs, 2, rows, n), F32),
             pltpu.VMEM((zs, 2 * heads, n), F32),
-            pltpu.VMEM((2, G, 2, rows, n), BF),
-            pltpu.VMEM((2, G, 2, rows, n), BF),
+            pltpu.VMEM((2, G, 2, rows, n), F32),
+            pltpu.VMEM((2, G, 2, rows, n), F32),
             pltpu.VMEM((heads, frames, frames), BF),
-            pltpu.VMEM((zs, Y, C, cut, wide), BF),
-            pltpu.VMEM((C, zs, Y, cut, wide), BF),
-            pltpu.VMEM((Y, zs, cut, wide), BF),
-            pltpu.VMEM((Y, zs, cut, wide), BF),
-            pltpu.VMEM((zs, cut, wide), BF),
-            pltpu.VMEM((zs, cut, wide), BF),
+            pltpu.VMEM((2, zs, Y, C, cut, wide // 2), BF),
+            pltpu.VMEM((2, C, zs, Y, cut, wide // 2), BF),
+            pltpu.VMEM((2, Y, zs, cut, wide // 2), BF),
+            pltpu.VMEM((2, Y, zs, cut, wide // 2), BF),
+            pltpu.VMEM((2, zs, cut, wide // 2), BF),
+            pltpu.VMEM((2, zs, cut, wide // 2), BF),
             pltpu.VMEM((frames, 4 * n), BF),
             pltpu.VMEM((groups, frames, 4 * n), BF),
             pltpu.VMEM((groups, frames, wide), BF),
             pltpu.VMEM((groups, frames, wide), BF),
-            pltpu.SemaphoreType.DMA((26,)),
+            pltpu.SemaphoreType.DMA((32,)),
         ],
         compiler_params=pltpu.CompilerParams(collective_id=0, has_side_effects=True),
     )(*args)
+    return pl.pallas_call(
+        hand_over, out_shape=shapes, in_specs=[vmem] * 8, out_specs=[vmem] * 8
+    )(*results)
 
 
 def solution(mesh):

time: 62 us -> 61.7 us (level)
  local copies, waits for them, and re-layouts: 6.62 us -> 0 us
  Pallas kernels: 54.3 us -> 60.9 us
    unnamed x22 -> x0, local copies, waits for them, and re-layouts: 6.62 us -> none
    pallas_call x1, Pallas kernels: 54.3 us -> 59.1 us  [local(): pl.pallas_call(functools.partial(layer_kernel, zs, heads, scale), out_sha...]
    pallas_call x0 -> x1, Pallas kernels: none -> 1.72 us  [local(): pl.pallas_call(hand_over, out_shape=shapes, in_specs=[vmem] * 8, out_spec...]
where the time goes in v3:
time: 61.7 us; the launch traced here: 61.5 us
  Pallas kernels  60.9 us (99%)
  between operations  0.64 us (1%)
    pallas_call x1, Pallas kernels, local(): pl.pallas_call(functools.partial(layer_kernel, zs, heads, scale), out_sha...  59.1 us
    pallas_call x1, Pallas kernels, local(): pl.pallas_call(hand_over, out_shape=shapes, in_specs=[vmem] * 8, out_spec...  1.72 us

profile of v3, /device:TPU:1, one launch (start us, length us, event | category | flops | bytes accessed | tf_op | source)
XLA Modules:
  0.0 61.5 jit_solution(17227248309194696583)
XLA Ops:
  0.6 59.1 %shard_map.161 = (bf16[128,256]{1,0:T(8,128)(2,1)}, f32[8,256]{1,0:T(8,128)}, f32[128,128]{1,0:T(8,128)}, f32[128,128]{1,0:T(8,128)}, f32[128,128]{1,0:T(8,128)}...) custom-call(bf16[128,1024]{1,0:T(8,128)(2,1)} %x_ref.1, bf16[1024,256]{1,0:T(8,128)(2,1)} %w_ref.1, ...), custom_call_target="tpu_custom_call" | custom-call | tf_op jit(solution)/shard_map/pallas_call | solution.py:334
  59.8 1.7 %shard_map.162 = (bf16[128,256]{1,0:T(8,128)(2,1)}, f32[8,256]{1,0:T(8,128)}, f32[128,128]{1,0:T(8,128)}, f32[128,128]{1,0:T(8,128)}, f32[128,128]{1,0:T(8,128)}...) custom-call(bf16[128,256]{1,0:T(8,128)(2,1)} %get-tuple-element.16.refs_0_, ...), custom_call_target="tpu_custom_call" | custom-call | tf_op jit(solution)/shard_map/pallas_call | solution.py:365
